TPU v7x, 128 devices: a whole 4x4x4 slice. The times are simulated.
128 devices in a mesh: row: 8 (over y, z_lo), col: 16 (over z_hi, x, core).
Axes of the slice: x: 4, y: 4, z: 4 (z_hi: 2, z_lo: 2; z = z_hi * 2 + z_lo), core: 2. Of those that a mesh axis runs over, the one named last changes fastest.
Arguments:
- kernel: bfloat16 [20480, 20480], P('row', 'col'), may hold values from -2.861023e-06 to 2.861023e-06
- occ: bfloat16 [20480, 128], P(('row', 'col')), may hold values from -6 to 6
- virt: bfloat16 [20480, 512], P(('col', 'row')), may hold values from -6 to 6
- rhs: float32 [128, 512], replicated, may hold values from -6 to 6
- e_occ: float32 [128], replicated, may hold values from -2 to -0.5
- e_virt: float32 [512], replicated, may hold values from 0.2 to 3
Outputs:
- amplitudes: float32 [128, 512], replicated
All inputs are finite; a program needn't handle non-finite values.
Results may differ from a plain program's by a relative error of at most 0.0045.
Values may be sent and summed in bfloat16 or wider, within the bound.
No kernel may reach another device: no remote copies, remote signals or barrier semaphores. Data moves between devices by JAX's collectives and lax.ppermute only.
A program may use at most 64 MiB of HBM per device.

v0:
```python
import functools

import jax
import jax.numpy as jnp
from jax import lax
from jax.experimental import pallas as pl
from jax.experimental.pallas import tpu as pltpu
from jax.sharding import PartitionSpec as P


ITERS = 2
LANES = 128
TALL = 512
BOTH = ("row", "col")
SEQUENCE = (3, 5, 2, 6, 7, 0, 1, 4)
NT = (((1,), (1,)), ((), ()))
TN = (((0,), (0,)), ((), ()))
VMEM = pl.BlockSpec(memory_space=pltpu.VMEM)
SMEM = pl.BlockSpec(memory_space=pltpu.SMEM)
HBM = pl.BlockSpec(memory_space=pltpu.HBM)


def sent_to_all(shard, axis):
    peers = lax.axis_size(axis)
    return lax.all_to_all(
        jnp.broadcast_to(shard[None], (peers, *shard.shape)), axis, 0, 0, tiled=True
    )


def place_kernel(axis, order, held_ref, out_ref):
    mine, tall = lax.axis_index(axis), held_ref.shape[1]
    for m, k in enumerate(order):
        start = pl.multiple_of(jnp.bitwise_xor(mine, m) * tall, tall)
        out_ref[pl.ds(start, tall), :] = held_ref[k]


def gathered_by_hops(source, shard, axis, masks):
    peers = lax.axis_size(axis)
    held, known = shard[None], [0]
    for stage, mask in enumerate(masks):
        sent = held if stage else source[None]
        other = lax.ppermute(sent, axis, [(i, i ^ mask) for i in range(peers)])
        held = jnp.concatenate([held, other], 0)
        known = known + [k ^ mask for k in known]
    order = [known.index(m) for m in range(peers)]
    return pl.pallas_call(
        functools.partial(place_kernel, axis, order),
        out_shape=jax.ShapeDtypeStruct((peers * shard.shape[0], shard.shape[1]), shard.dtype),
        in_specs=[VMEM],
        out_specs=VMEM,
        compiler_params=pltpu.CompilerParams(vmem_limit_bytes=4 << 20),
    )(held)


def gathered_by_rows(copies):
    cols = lax.axis_size("col")
    groups = [[row * cols + col for row in SEQUENCE] for col in range(cols)]
    return lax.all_to_all(copies, BOTH, 0, 0, tiled=True, axis_index_groups=groups)


def stage_kernel(
    virt_ref, occ_ref, rhs_ref, e_occ_ref, e_virt_ref,
    copies_ref, occ_out_ref, amp_ref, rhs_mine_ref, denom_mine_ref,
    virt_here, rhs_here, e_occ_here, e_virt_here, denom_here, sem_in, sem_out,
):
    pairs = (
        (virt_ref, virt_here),
        (rhs_ref, rhs_here),
        (e_occ_ref, e_occ_here),
        (e_virt_ref, e_virt_here),
        (occ_ref, occ_out_ref),
    )
    fetches = [pltpu.make_async_copy(*pair, sem_in.at[i]) for i, pair in enumerate(pairs)]
    for fetch in fetches:
        fetch.start()
    fetches[0].wait()
    sends = [
        pltpu.make_async_copy(virt_here, copies_ref.at[peer], sem_out.at[peer])
        for peer in range(copies_ref.shape[0])
    ]
    for send in sends:
        send.start()
    for fetch in fetches[1:]:
        fetch.wait()
    denom = e_virt_here[...] - e_occ_here[...].T
    denom_here[...] = denom
    amp_ref[...] = (rhs_here[...] / denom).astype(amp_ref.dtype)
    tall, lanes = denom_mine_ref.shape
    parts = rhs_here.shape[1] // lanes
    mine = lax.axis_index("row") * lax.axis_size("col") + lax.axis_index("col")
    group, part = mine // parts, mine % parts
    rows = pl.ds(pl.multiple_of(group // 2 * (2 * tall), 2 * tall), 2 * tall)
    columns = pl.ds(pl.multiple_of(part * lanes, lanes), lanes)
    for from_ref, to_ref in ((rhs_here, rhs_mine_ref), (denom_here, denom_mine_ref)):
        pair = from_ref[rows, columns]
        to_ref[...] = jnp.where(group % 2 == 0, pair[:tall], pair[tall:])
    for send in sends:
        send.wait()


def staged(virt, occ, rhs, e_occ, e_virt, tall):
    f32, b16 = jnp.float32, jnp.bfloat16
    peers = lax.axis_size("row")
    small = jax.ShapeDtypeStruct((tall, LANES), f32)
    args = [
        pltpu.with_memory_space_constraint(array, pltpu.HBM)
        for array in (virt, occ, rhs, e_occ.reshape(1, -1), e_virt.reshape(1, -1))
    ]
    return pl.pallas_call(
        stage_kernel,
        out_shape=(
            jax.ShapeDtypeStruct((peers, *virt.shape), b16),
            jax.ShapeDtypeStruct(occ.shape, b16),
            jax.ShapeDtypeStruct(rhs.shape, b16),
            small,
            small,
        ),
        in_specs=[HBM] * 5,
        out_specs=(HBM, VMEM, VMEM, VMEM, VMEM),
        scratch_shapes=[
            pltpu.VMEM(virt.shape, b16),
            pltpu.VMEM(rhs.shape, f32),
            pltpu.VMEM((1, rhs.shape[0]), f32),
            pltpu.VMEM((1, rhs.shape[1]), f32),
            pltpu.VMEM(rhs.shape, f32),
            pltpu.SemaphoreType.DMA((5,)),
            pltpu.SemaphoreType.DMA((peers,)),
        ],
        compiler_params=pltpu.CompilerParams(vmem_limit_bytes=4 << 20),
    )(*args)


def head_kernel(kern_ref, head_ref, sem):
    copy = pltpu.make_async_copy(kern_ref.at[pl.ds(0, head_ref.shape[0])], head_ref, sem)
    copy.start()
    copy.wait()


def head_of(kernel):
    return pl.pallas_call(
        head_kernel,
        out_shape=jax.ShapeDtypeStruct((TALL, kernel.shape[1]), kernel.dtype),
        in_specs=[HBM],
        out_specs=VMEM,
        scratch_shapes=[pltpu.SemaphoreType.DMA],
        compiler_params=pltpu.CompilerParams(vmem_limit_bytes=1 << 20),
    )(pltpu.with_memory_space_constraint(kernel, pltpu.HBM))


def put_together(blocks_ref, out_ref):
    count, tall, lanes = blocks_ref.shape
    parts = out_ref.shape[1] // lanes
    for block in range(count):
        row, column = block // parts * tall, block % parts * lanes
        out_ref[row : row + tall, column : column + lanes] = blocks_ref[block].astype(out_ref.dtype)


def last_kernel(blocks_ref, rhs_ref, e_occ_ref, e_virt_ref, out_ref, exchange_ref):
    put_together(blocks_ref, exchange_ref)
    denom = e_virt_ref[...] - e_occ_ref[...].T
    out_ref[...] = (rhs_ref[...] - exchange_ref[...]) / denom


def last_amplitudes(blocks, rhs, e_occ, e_virt):
    return pl.pallas_call(
        last_kernel,
        out_shape=jax.ShapeDtypeStruct(rhs.shape, jnp.float32),
        in_specs=[VMEM] * 4,
        scratch_shapes=[pltpu.VMEM(rhs.shape, jnp.float32)],
        compiler_params=pltpu.CompilerParams(vmem_limit_bytes=4 << 20),
    )(blocks, rhs, e_occ.reshape(1, -1), e_virt.reshape(1, -1))


def response_kernel(cuts, amp_ref, virt_ref, occ_ref, head_ref, kern_ref, out_ref, *held):
    f32, b16 = jnp.float32, jnp.bfloat16
    tall = head_ref.shape[0]
    blocks = occ_ref.shape[0] // tall
    waits = {}
    if cuts:
        rest_ref, ordered_ref, sem = held
        for i, (first, last) in enumerate(zip(cuts, (*cuts[1:], blocks))):
            size = (last - first) * tall
            waits[first] = pltpu.make_async_copy(
                kern_ref.at[pl.ds(first * tall, size)],
                rest_ref.at[pl.ds((first - 1) * tall, size)],
                sem.at[i],
            )
            waits[first].start()
        share = virt_ref.shape[1]
        for i, row in enumerate(SEQUENCE):
            ordered_ref[row * share : (row + 1) * share, :] = virt_ref[i]
        kern_ref, virt_ref = rest_ref, ordered_ref
    else:
        (joined_ref,) = held
        put_together(amp_ref, joined_ref)
        amp_ref = joined_ref
    w = lax.dot_general(amp_ref[...], virt_ref[...], NT, preferred_element_type=f32).astype(b16)

    def outer_of(block):
        return jnp.dot(occ_ref[pl.ds(block * tall, tall), :], w, preferred_element_type=f32)

    ahead, contracted = outer_of(0), None
    for block in range(blocks):
        here = pl.ds(block * tall, tall)
        if block in waits:
            waits[block].wait()
        outer = ahead
        if block + 1 < blocks:
            ahead = outer_of(block + 1)
        rows_here = kern_ref[pl.ds((block - 1) * tall, tall), :] if block else head_ref[...]
        weighted = (rows_here.astype(f32) * outer).astype(b16)
        more = lax.dot_general(occ_ref[here, :], weighted, TN, preferred_element_type=f32)
        contracted = more if contracted is None else contracted + more
    high = contracted.astype(b16)
    low = (contracted - high.astype(f32)).astype(b16)
    exchange = jnp.dot(high, virt_ref[...], preferred_element_type=f32)
    exchange += jnp.dot(low, virt_ref[...], preferred_element_type=f32)
    _, rows, lanes = out_ref.shape
    parts = exchange.shape[1] // lanes
    for group in range(exchange.shape[0] // rows):
        for part in range(parts):
            out_ref[group * parts + part] = exchange[
                group * rows : (group + 1) * rows, part * lanes : (part + 1) * lanes
            ].astype(out_ref.dtype)


def first_exchange(amp_b, virt_blocks, occ_rows, head, kernel, pieces):
    peers, share, virtual = virt_blocks.shape
    cuts, b16 = (1, 3), jnp.bfloat16
    return pl.pallas_call(
        functools.partial(response_kernel, cuts),
        out_shape=(
            jax.ShapeDtypeStruct(pieces, b16),
            jax.ShapeDtypeStruct((kernel.shape[0] - head.shape[0], kernel.shape[1]), b16),
            jax.ShapeDtypeStruct((peers * share, virtual), b16),
        ),
        in_specs=[VMEM, VMEM, VMEM, VMEM, HBM],
        out_specs=(VMEM, VMEM, VMEM),
        scratch_shapes=[pltpu.SemaphoreType.DMA((len(cuts),))],
        compiler_params=pltpu.CompilerParams(vmem_limit_bytes=40 << 20),
    )(amp_b, virt_blocks, occ_rows, head, pltpu.with_memory_space_constraint(kernel, pltpu.HBM))


def next_exchange(amp_blocks, virt_cols, occ_rows, head, rest):
    return pl.pallas_call(
        functools.partial(response_kernel, ()),
        out_shape=jax.ShapeDtypeStruct(amp_blocks.shape, jnp.bfloat16),
        in_specs=[VMEM] * 5,
        out_specs=VMEM,
        scratch_shapes=[pltpu.VMEM((occ_rows.shape[1], virt_cols.shape[1]), jnp.bfloat16)],
        compiler_params=pltpu.CompilerParams(vmem_limit_bytes=40 << 20),
    )(amp_blocks, virt_cols, occ_rows, head, rest)


def body(kernel, occ, virt, rhs, e_occ, e_virt):
    occupied, virtual = rhs.shape
    devices = lax.axis_size(BOTH)
    pieces = (devices, occupied * virtual // (devices * LANES), LANES)
    copies, occ_here, amp_b, rhs_mine, denom_mine = staged(
        virt, occ, rhs, e_occ, e_virt, pieces[1]
    )
    virt_blocks = gathered_by_rows(copies)
    occ_rows = gathered_by_hops(occ, occ_here, "col", (8, 4, 2, 1))
    head = head_of(kernel)

    for step in range(ITERS):
        if step == 0:
            part, rest, virt_cols = first_exchange(
                amp_b, virt_blocks, occ_rows, head, kernel, pieces
            )
        else:
            part = next_exchange(amp_b, virt_cols, occ_rows, head, rest)
        parts = lax.all_to_all(part, BOTH, 0, 0, tiled=True)
        exchange = jnp.sum(parts.astype(jnp.float32), axis=0)
        if step < ITERS - 1:
            amp_mine = (rhs_mine - exchange) / denom_mine
            amp_b = sent_to_all(amp_mine.astype(jnp.bfloat16), BOTH)
    return last_amplitudes(sent_to_all(exchange.astype(jnp.bfloat16), BOTH), rhs, e_occ, e_virt)


def solution(mesh):
    in_specs = (P("row", "col"), P(("row", "col"), None), P(("col", "row"), None), P(), P(), P())
    return jax.shard_map(body, mesh=mesh, in_specs=in_specs, out_specs=P(), check_vma=False)
```

profile of v0, /device:TPU:1, one launch (start us, length us, event | category | flops | bytes accessed | tf_op | source)
XLA Modules:
  0.0 97.2 jit_solution(15324182357087137624)
XLA Ops:
  0.0 4.4 %collective-permute-start = (bf16[1,160,128]{2,1,0:T(8,128)(2,1)}, bf16[1,160,128]{2,1,0:T(8,128)(2,1)S(1)}, u32[]{:S(2)}, u32[]{:S(2)}) collective-permute-start(bf16[1,160,128]{2,1,0:T(8,128)(2,1)} %bitcast.12), channel_id=1, source_target_pairs={{0,8},{1,9},{2,10},{3,11},{4,12},{5,13},{6,14},{7,15},{8,0},{9,1},... | collective-permute-start | bytes 122888 | tf_op jit(solution)/shard_map/ppermute | solution.py:42
  4.4 2.1 %shard_map.64 = (bf16[8,160,512]{2,1,0:T(8,128)(2,1)}, bf16[160,128]{1,0:T(8,128)(2,1)S(1)}, bf16[128,512]{1,0:T(8,128)(2,1)S(1)}, f32[4,128]{1,0:T(4,128)S(1)}, f32[4,128]{1,0:T(4,128)S(1)}) custom-call(bf16[160,512]{1,0:T(8,128)(2,1)} %virt_ref.1, bf16[160,128]{1,0:T(8,128)(2,1)} %occ_ref.1, f32[128,512]{1,0:T(8,128)} %rhs_ref.3, f32[1,128]{1,0:T(1,128)} %bitcast.10, ...), custom_call_target="tpu_custom_call" | custom-call | tf_op jit(solution)/shard_map/pallas_call | solution.py:109
  6.5 5.5 %all-to-all-start = ((bf16[8,160,512]{2,1,0:T(8,128)(2,1)}), bf16[8,160,512]{2,1,0:T(8,128)(2,1)S(1)}, u32[]{:S(2)}, u32[]{:S(2)}) async-start(bf16[8,160,512]{2,1,0:T(8,128)(2,1)} %get-tuple-element.15), calls=%async_computation | async-start | bytes 2621440 | tf_op jit(solution)/shard_map/all_to_all | solution.py:58
  12.0 0.0 collective-permute-done
  12.0 2.8 %collective-permute-start.1 = (bf16[2,160,128]{2,1,0:T(8,128)(2,1)S(1)}, bf16[2,160,128]{2,1,0:T(8,128)(2,1)S(1)}, u32[]{:S(2)}, u32[]{:S(2)}) collective-permute-start(bf16[2,160,128]{2,1,0:T(8,128)(2,1)S(1)} %pad_maximum_fusion.2), channel_id=1, source_target_pairs={{0,4},{1,5},{2,6},{3,7},{4,0},{5,1},{6,2},{7,3},{8,12},{9,13},{10,... | collective-permute-start | bytes 245768 | tf_op jit(solution)/shard_map/ppermute | solution.py:42
  14.9 1.3 %shard_map.66.head_ref = bf16[512,1280]{1,0:T(8,128)(2,1)S(1)} custom-call(bf16[2560,1280]{1,0:T(8,128)(2,1)} %kern_ref.3), custom_call_target="tpu_custom_call" | custom-call | tf_op jit(solution)/shard_map/pallas_call | solution.py:140
  16.2 0.7 collective-permute-done.1
  16.9 1.3 %collective-permute-start.2 = (bf16[4,160,128]{2,1,0:T(8,128)(2,1)S(1)}, bf16[4,160,128]{2,1,0:T(8,128)(2,1)S(1)}, u32[]{:S(2)}, u32[]{:S(2)}) collective-permute-start(bf16[4,160,128]{2,1,0:T(8,128)(2,1)S(1)} %pad_maximum_fusion.1), channel_id=1, source_target_pairs={{0,2},{1,3},{2,0},{3,1},{4,6},{5,7},{6,4},{7,5},{8,10},{9,11},{10,... | collective-permute-start | bytes 491528 | tf_op jit(solution)/shard_map/ppermute | solution.py:42
  18.2 3.2 %collective-permute-done.2 = bf16[4,160,128]{2,1,0:T(8,128)(2,1)S(1)} collective-permute-done((bf16[4,160,128]{2,1,0:T(8,128)(2,1)S(1)}, bf16[4,160,128]{2,1,0:T(8,128)(2,1)S(1)}, u32[]{:S(2)}, u32[]{:S(2)}) %collective-permute-start.2) | collective-permute-done | bytes 163872 | tf_op jit(solution)/shard_map/ppermute | solution.py:42
  21.5 3.6 %collective-permute-start.3 = (bf16[8,160,128]{2,1,0:T(8,128)(2,1)S(1)}, bf16[8,160,128]{2,1,0:T(8,128)(2,1)S(1)}, u32[]{:S(2)}, u32[]{:S(2)}) collective-permute-start(bf16[8,160,128]{2,1,0:T(8,128)(2,1)S(1)} %pad_maximum_fusion), channel_id=1, source_target_pairs={{0,1},{1,0},{2,3},{3,2},{4,5},{5,4},{6,7},{7,6},{8,9},{9,8},{10,11... | collective-permute-start | bytes 983048 | tf_op jit(solution)/shard_map/ppermute | solution.py:42
  25.2 1.2 %collective-permute-done.3 = bf16[8,160,128]{2,1,0:T(8,128)(2,1)S(1)} collective-permute-done((bf16[8,160,128]{2,1,0:T(8,128)(2,1)S(1)}, bf16[8,160,128]{2,1,0:T(8,128)(2,1)S(1)}, u32[]{:S(2)}, u32[]{:S(2)}) %collective-permute-start.3) | collective-permute-done | bytes 327712 | tf_op jit(solution)/shard_map/ppermute | solution.py:42
  26.4 0.1 shard_map.65.occ_ref
  26.5 2.7 %all-to-all-done.virt_ref = bf16[8,160,512]{2,1,0:T(8,128)(2,1)S(1)} async-done(((bf16[8,160,512]{2,1,0:T(8,128)(2,1)}), bf16[8,160,512]{2,1,0:T(8,128)(2,1)S(1)}, u32[]{:S(2)}, u32[]{:S(2)}) %all-to-all-start) | async-done | bytes 1310752 | tf_op jit(solution)/shard_map/all_to_all | solution.py:58
  29.2 4.4 %shard_map.67 = (bf16[128,4,128]{2,1,0:T(4,128)(2,1)S(1)}, bf16[2048,1280]{1,0:T(8,128)(2,1)S(1)}, bf16[1280,512]{1,0:T(8,128)(2,1)S(1)}) custom-call(bf16[128,512]{1,0:T(8,128)(2,1)S(1)} %get-tuple-element.14.amp_ref, bf16[8,160,512]{2,1,0:T(8,128)(2,1)S(1)} %all-to-all-done.virt_ref, bf16[2560,128]{1,0:T(8,128)(2,1)S(1)} %shard_map.65.occ_ref, ...), custom_call_target="tpu_custom_call" | custom-call | tf_op jit(solution)/shard_map/pallas_call | solution.py:230
  33.6 16.4 %all_to_all.25 = bf16[128,4,128]{2,1,0:T(4,128)(2,1)S(1)} all-to-all(bf16[128,4,128]{2,1,0:T(4,128)(2,1)S(1)} %get-tuple-element.17), channel_id=1, replica_groups=mesh['row'=8,'col'=16] {'row','col'}, dimensions={0} | all-to-all | bytes 262144 | tf_op jit(solution)/shard_map/all_to_all | solution.py:273
  50.0 0.1 convert_reduce_fusion
  50.2 14.2 %all_to_all.26.amp_ref = bf16[128,4,128]{2,1,0:T(4,128)(2,1)S(1)} all-to-all(bf16[128,4,128]{2,1,0:T(4,128)(2,1)S(1)} %broadcast_in_dim.20), channel_id=1, replica_groups=mesh['row'=8,'col'=16] {'row','col'}, dimensions={0} | all-to-all | bytes 262144 | tf_op jit(solution)/shard_map/all_to_all | solution.py:25
  64.3 0.0 copy-start
  64.3 0.0 copy-start.1
  64.3 0.0 copy-start.2
  64.3 3.5 %shard_map.68 = bf16[128,4,128]{2,1,0:T(4,128)(2,1)S(1)} custom-call(bf16[128,4,128]{2,1,0:T(4,128)(2,1)S(1)} %all_to_all.26.amp_ref, bf16[1280,512]{1,0:T(8,128)(2,1)S(1)} %get-tuple-element.19.virt_ref, bf16[2560,128]{1,0:T(8,128)(2,1)S(1)} %shard_map.65.occ_ref, bf16[512,1280]{1,0:T(8,128)(2,1)S(1)} %shard_map.66.head_ref, ...), custom_call_target="tpu_custom_call" | custom-call | tf_op jit(solution)/shard_map/pallas_call | solution.py:245
  67.8 14.2 %all_to_all.27 = bf16[128,4,128]{2,1,0:T(4,128)(2,1)S(1)} all-to-all(bf16[128,4,128]{2,1,0:T(4,128)(2,1)S(1)} %shard_map.68), channel_id=1, replica_groups=mesh['row'=8,'col'=16] {'row','col'}, dimensions={0} | all-to-all | bytes 262144 | tf_op jit(solution)/shard_map/all_to_all | solution.py:273
  82.0 0.1 reduce_sum.22
  82.2 14.2 %all_to_all.28.blocks_ref = bf16[128,4,128]{2,1,0:T(4,128)(2,1)S(1)} all-to-all(bf16[128,4,128]{2,1,0:T(4,128)(2,1)S(1)} %broadcast_in_dim.21), channel_id=1, replica_groups=mesh['row'=8,'col'=16] {'row','col'}, dimensions={0} | all-to-all | bytes 262144 | tf_op jit(solution)/shard_map/all_to_all | solution.py:25
  96.3 0.0 copy-done
  96.3 0.0 copy-done.1
  96.3 0.0 copy-done.2
  96.3 0.9 shard_map.69
  (11 shorter events, 0.2 us)
Async XLA Ops:
  0.0 12.0 %collective-permute-start = (bf16[1,160,128]{2,1,0:T(8,128)(2,1)}, bf16[1,160,128]{2,1,0:T(8,128)(2,1)S(1)}, u32[]{:S(2)}, u32[]{:S(2)}) collective-permute-start(bf16[1,160,128]{2,1,0:T(8,128)(2,1)} %bitcast.12), channel_id=1, source_target_pairs={{0,8},{1,9},{2,10},{3,11},{4,12},{5,13},{6,14},{7,15},{8,0},{9,1},... | collective-permute-start | bytes 122888 | tf_op jit(solution)/shard_map/ppermute | solution.py:42
  6.5 22.7 %all-to-all-start = ((bf16[8,160,512]{2,1,0:T(8,128)(2,1)}), bf16[8,160,512]{2,1,0:T(8,128)(2,1)S(1)}, u32[]{:S(2)}, u32[]{:S(2)}) async-start(bf16[8,160,512]{2,1,0:T(8,128)(2,1)} %get-tuple-element.15), calls=%async_computation | async-start | bytes 2621440 | tf_op jit(solution)/shard_map/all_to_all | solution.py:58
  12.0 4.9 %collective-permute-start.1 = (bf16[2,160,128]{2,1,0:T(8,128)(2,1)S(1)}, bf16[2,160,128]{2,1,0:T(8,128)(2,1)S(1)}, u32[]{:S(2)}, u32[]{:S(2)}) collective-permute-start(bf16[2,160,128]{2,1,0:T(8,128)(2,1)S(1)} %pad_maximum_fusion.2), channel_id=1, source_target_pairs={{0,4},{1,5},{2,6},{3,7},{4,0},{5,1},{6,2},{7,3},{8,12},{9,13},{10,... | collective-permute-start | bytes 245768 | tf_op jit(solution)/shard_map/ppermute | solution.py:42
  16.9 4.5 %collective-permute-start.2 = (bf16[4,160,128]{2,1,0:T(8,128)(2,1)S(1)}, bf16[4,160,128]{2,1,0:T(8,128)(2,1)S(1)}, u32[]{:S(2)}, u32[]{:S(2)}) collective-permute-start(bf16[4,160,128]{2,1,0:T(8,128)(2,1)S(1)} %pad_maximum_fusion.1), channel_id=1, source_target_pairs={{0,2},{1,3},{2,0},{3,1},{4,6},{5,7},{6,4},{7,5},{8,10},{9,11},{10,... | collective-permute-start | bytes 491528 | tf_op jit(solution)/shard_map/ppermute | solution.py:42
  21.5 4.9 %collective-permute-start.3 = (bf16[8,160,128]{2,1,0:T(8,128)(2,1)S(1)}, bf16[8,160,128]{2,1,0:T(8,128)(2,1)S(1)}, u32[]{:S(2)}, u32[]{:S(2)}) collective-permute-start(bf16[8,160,128]{2,1,0:T(8,128)(2,1)S(1)} %pad_maximum_fusion), channel_id=1, source_target_pairs={{0,1},{1,0},{2,3},{3,2},{4,5},{5,4},{6,7},{7,6},{8,9},{9,8},{10,11... | collective-permute-start | bytes 983048 | tf_op jit(solution)/shard_map/ppermute | solution.py:42
  64.3 32.0 %copy-start = (f32[128,512]{1,0:T(8,128)S(1)}, f32[128,512]{1,0:T(8,128)}, u32[]{:S(2)}) copy-start(f32[128,512]{1,0:T(8,128)} %rhs_ref.3) | copy-start | bytes 786436
  64.3 32.0 %copy-start.1 = (f32[512]{0:T(512)S(1)}, f32[512]{0:T(512)}, u32[]{:S(2)}) copy-start(f32[512]{0:T(512)} %param.11) | copy-start | bytes 6148
  64.3 32.0 %copy-start.2 = (f32[128]{0:T(128)S(1)}, f32[128]{0:T(128)}, u32[]{:S(2)}) copy-start(f32[128]{0:T(128)} %param.10) | copy-start | bytes 1540
where the time goes:
time: 97.5 us; the launch traced here: 97.2 us
  blocking collectives  58.8 us (60%)
  starting transfers between devices  17.6 us (18%)
  Pallas kernels  12.2 us (13%)
  waiting for transfers between devices  7.88 us (8%)
    all_to_all x2, blocking collectives, body(): parts = lax.all_to_all(part, BOTH, 0, 0, tiled=True)  30.5 us
    all_to_all x2, blocking collectives, sent_to_all(): lax.all_to_all(jnp.broadcast_to(shard[None], (peers, *shard.shape)), axis...  28.3 us
    ppermute x4, starting transfers between devices, gathered_by_hops(): other = lax.ppermute(sent, axis, [(i, i ^ mask) for i in range(peers)])  12.1 us
    all_to_all x1, starting transfers between devices, gathered_by_rows(): lax.all_to_all(copies, BOTH, 0, 0, tiled=True, axis_index_groups=groups)  5.5 us
    ppermute x4, waiting for transfers between devices, gathered_by_hops(): other = lax.ppermute(sent, axis, [(i, i ^ mask) for i in range(peers)])  5.17 us
    pallas_call x1, Pallas kernels, first_exchange(): pl.pallas_call(functools.partial(response_kernel, cuts), out_shape=(jax.S...  4.37 us
    pallas_call x1, Pallas kernels, next_exchange(): pl.pallas_call(functools.partial(response_kernel, ()), out_shape=jax.Shap...  3.51 us
    all_to_all x1, waiting for transfers between devices, gathered_by_rows(): lax.all_to_all(copies, BOTH, 0, 0, tiled=True, axis_index_groups=groups)  2.71 us
  transfers between devices with their start and end apart: 5, of which 4 were waited for; matrix products, arithmetic and copies ran while one was open for 0% of the time, Pallas kernels for 4%

commit v1 on v0

--- a/solution.py
+++ b/solution.py
@@ -12,7 +12,7 @@
 LANES = 128
 TALL = 512
 BOTH = ("row", "col")
-SEQUENCE = (3, 5, 2, 6, 7, 0, 1, 4)
+SEQUENCE = (2, 4, 3, 7, 6, 1, 0, 5)
 NT = (((1,), (1,)), ((), ()))
 TN = (((0,), (0,)), ((), ()))
 VMEM = pl.BlockSpec(memory_space=pltpu.VMEM)
@@ -213,8 +213,8 @@
         contracted = more if contracted is None else contracted + more
     high = contracted.astype(b16)
     low = (contracted - high.astype(f32)).astype(b16)
-    exchange = jnp.dot(high, virt_ref[...], preferred_element_type=f32)
-    exchange += jnp.dot(low, virt_ref[...], preferred_element_type=f32)
+    both = jnp.dot(jnp.concatenate([high, low], 0), virt_ref[...], preferred_element_type=f32)
+    exchange = both[: high.shape[0]] + both[high.shape[0] :]
     _, rows, lanes = out_ref.shape
     parts = exchange.shape[1] // lanes
     for group in range(exchange.shape[0] // rows):

time: 97.5 us -> 97.6 us (level)
  blocking collectives: 58.8 us -> 61.1 us
  waiting for transfers between devices: 7.88 us -> 6.19 us
    all_to_all x2, blocking collectives: 30.5 us -> 32.8 us  [body(): parts = lax.all_to_all(part, BOTH, 0, 0, tiled=True)]
    all_to_all x1, waiting for transfers between devices: 2.71 us -> 1.02 us  [gathered_by_rows(): lax.all_to_all(copies, BOTH, 0, 0, tiled=True, axis_index_groups=groups)]
where the time goes in v1:
time: 97.6 us; the launch traced here: 97.3 us
  blocking collectives  61.1 us (63%)
  starting transfers between devices  17.2 us (18%)
  Pallas kernels  12.2 us (12%)
  waiting for transfers between devices  6.19 us (6%)
    all_to_all x2, blocking collectives, body(): parts = lax.all_to_all(part, BOTH, 0, 0, tiled=True)  32.8 us
    all_to_all x2, blocking collectives, sent_to_all(): lax.all_to_all(jnp.broadcast_to(shard[None], (peers, *shard.shape)), axis...  28.3 us
    ppermute x4, starting transfers between devices, gathered_by_hops(): other = lax.ppermute(sent, axis, [(i, i ^ mask) for i in range(peers)])  12.1 us
    ppermute x4, waiting for transfers between devices, gathered_by_hops(): other = lax.ppermute(sent, axis, [(i, i ^ mask) for i in range(peers)])  5.17 us
    all_to_all x1, starting transfers between devices, gathered_by_rows(): lax.all_to_all(copies, BOTH, 0, 0, tiled=True, axis_index_groups=groups)  5.05 us
    pallas_call x1, Pallas kernels, first_exchange(): pl.pallas_call(functools.partial(response_kernel, cuts), out_shape=(jax.S...  4.36 us
    pallas_call x1, Pallas kernels, next_exchange(): pl.pallas_call(functools.partial(response_kernel, ()), out_shape=jax.Shap...  3.5 us
    pallas_call x1, Pallas kernels, staged(): pl.pallas_call(stage_kernel, out_shape=(jax.ShapeDtypeStruct((peers, *vir...  2.1 us
  transfers between devices with their start and end apart: 5, of which 4 were waited for; matrix products, arithmetic and copies ran while one was open for 0% of the time, Pallas kernels for 4%

profile of v1, /device:TPU:1, one launch (start us, length us, event | category | flops | bytes accessed | tf_op | source)
XLA Modules:
  0.0 97.3 jit_solution(343930173712135650)
XLA Ops:
  0.0 4.4 %collective-permute-start = (bf16[1,160,128]{2,1,0:T(8,128)(2,1)}, bf16[1,160,128]{2,1,0:T(8,128)(2,1)S(1)}, u32[]{:S(2)}, u32[]{:S(2)}) collective-permute-start(bf16[1,160,128]{2,1,0:T(8,128)(2,1)} %bitcast.12), channel_id=1, source_target_pairs={{0,8},{1,9},{2,10},{3,11},{4,12},{5,13},{6,14},{7,15},{8,0},{9,1},... | collective-permute-start | bytes 122888 | tf_op jit(solution)/shard_map/ppermute | solution.py:42
  4.4 2.1 %shard_map.64 = (bf16[8,160,512]{2,1,0:T(8,128)(2,1)}, bf16[160,128]{1,0:T(8,128)(2,1)S(1)}, bf16[128,512]{1,0:T(8,128)(2,1)S(1)}, f32[4,128]{1,0:T(4,128)S(1)}, f32[4,128]{1,0:T(4,128)S(1)}) custom-call(bf16[160,512]{1,0:T(8,128)(2,1)} %virt_ref.1, bf16[160,128]{1,0:T(8,128)(2,1)} %occ_ref.1, f32[128,512]{1,0:T(8,128)} %rhs_ref.3, f32[1,128]{1,0:T(1,128)} %bitcast.10, ...), custom_call_target="tpu_custom_call" | custom-call | tf_op jit(solution)/shard_map/pallas_call | solution.py:109
  6.5 5.1 %all-to-all-start = ((bf16[8,160,512]{2,1,0:T(8,128)(2,1)}), bf16[8,160,512]{2,1,0:T(8,128)(2,1)S(1)}, u32[]{:S(2)}, u32[]{:S(2)}) async-start(bf16[8,160,512]{2,1,0:T(8,128)(2,1)} %get-tuple-element.15), calls=%async_computation | async-start | bytes 2621440 | tf_op jit(solution)/shard_map/all_to_all | solution.py:58
  11.6 0.0 collective-permute-done
  11.6 2.8 %collective-permute-start.1 = (bf16[2,160,128]{2,1,0:T(8,128)(2,1)S(1)}, bf16[2,160,128]{2,1,0:T(8,128)(2,1)S(1)}, u32[]{:S(2)}, u32[]{:S(2)}) collective-permute-start(bf16[2,160,128]{2,1,0:T(8,128)(2,1)S(1)} %pad_maximum_fusion.2), channel_id=1, source_target_pairs={{0,4},{1,5},{2,6},{3,7},{4,0},{5,1},{6,2},{7,3},{8,12},{9,13},{10,... | collective-permute-start | bytes 245768 | tf_op jit(solution)/shard_map/ppermute | solution.py:42
  14.4 1.3 %shard_map.66.head_ref = bf16[512,1280]{1,0:T(8,128)(2,1)S(1)} custom-call(bf16[2560,1280]{1,0:T(8,128)(2,1)} %kern_ref.3), custom_call_target="tpu_custom_call" | custom-call | tf_op jit(solution)/shard_map/pallas_call | solution.py:140
  15.7 0.7 collective-permute-done.1
  16.5 1.3 %collective-permute-start.2 = (bf16[4,160,128]{2,1,0:T(8,128)(2,1)S(1)}, bf16[4,160,128]{2,1,0:T(8,128)(2,1)S(1)}, u32[]{:S(2)}, u32[]{:S(2)}) collective-permute-start(bf16[4,160,128]{2,1,0:T(8,128)(2,1)S(1)} %pad_maximum_fusion.1), channel_id=1, source_target_pairs={{0,2},{1,3},{2,0},{3,1},{4,6},{5,7},{6,4},{7,5},{8,10},{9,11},{10,... | collective-permute-start | bytes 491528 | tf_op jit(solution)/shard_map/ppermute | solution.py:42
  17.8 3.2 %collective-permute-done.2 = bf16[4,160,128]{2,1,0:T(8,128)(2,1)S(1)} collective-permute-done((bf16[4,160,128]{2,1,0:T(8,128)(2,1)S(1)}, bf16[4,160,128]{2,1,0:T(8,128)(2,1)S(1)}, u32[]{:S(2)}, u32[]{:S(2)}) %collective-permute-start.2) | collective-permute-done | bytes 163872 | tf_op jit(solution)/shard_map/ppermute | solution.py:42
  21.1 3.6 %collective-permute-start.3 = (bf16[8,160,128]{2,1,0:T(8,128)(2,1)S(1)}, bf16[8,160,128]{2,1,0:T(8,128)(2,1)S(1)}, u32[]{:S(2)}, u32[]{:S(2)}) collective-permute-start(bf16[8,160,128]{2,1,0:T(8,128)(2,1)S(1)} %pad_maximum_fusion), channel_id=1, source_target_pairs={{0,1},{1,0},{2,3},{3,2},{4,5},{5,4},{6,7},{7,6},{8,9},{9,8},{10,11... | collective-permute-start | bytes 983048 | tf_op jit(solution)/shard_map/ppermute | solution.py:42
  24.7 1.2 %collective-permute-done.3 = bf16[8,160,128]{2,1,0:T(8,128)(2,1)S(1)} collective-permute-done((bf16[8,160,128]{2,1,0:T(8,128)(2,1)S(1)}, bf16[8,160,128]{2,1,0:T(8,128)(2,1)S(1)}, u32[]{:S(2)}, u32[]{:S(2)}) %collective-permute-start.3) | collective-permute-done | bytes 327712 | tf_op jit(solution)/shard_map/ppermute | solution.py:42
  26.0 0.1 shard_map.65.occ_ref
  26.0 1.0 %all-to-all-done.virt_ref = bf16[8,160,512]{2,1,0:T(8,128)(2,1)S(1)} async-done(((bf16[8,160,512]{2,1,0:T(8,128)(2,1)}), bf16[8,160,512]{2,1,0:T(8,128)(2,1)S(1)}, u32[]{:S(2)}, u32[]{:S(2)}) %all-to-all-start) | async-done | bytes 1310752 | tf_op jit(solution)/shard_map/all_to_all | solution.py:58
  27.1 4.4 %shard_map.67 = (bf16[128,4,128]{2,1,0:T(4,128)(2,1)S(1)}, bf16[2048,1280]{1,0:T(8,128)(2,1)S(1)}, bf16[1280,512]{1,0:T(8,128)(2,1)S(1)}) custom-call(bf16[128,512]{1,0:T(8,128)(2,1)S(1)} %get-tuple-element.14.amp_ref, bf16[8,160,512]{2,1,0:T(8,128)(2,1)S(1)} %all-to-all-done.virt_ref, bf16[2560,128]{1,0:T(8,128)(2,1)S(1)} %shard_map.65.occ_ref, ...), custom_call_target="tpu_custom_call" | custom-call | tf_op jit(solution)/shard_map/pallas_call | solution.py:230
  31.4 18.6 %all_to_all.25 = bf16[128,4,128]{2,1,0:T(4,128)(2,1)S(1)} all-to-all(bf16[128,4,128]{2,1,0:T(4,128)(2,1)S(1)} %get-tuple-element.17), channel_id=1, replica_groups=mesh['row'=8,'col'=16] {'row','col'}, dimensions={0} | all-to-all | bytes 262144 | tf_op jit(solution)/shard_map/all_to_all | solution.py:273
  50.1 0.1 convert_reduce_fusion
  50.3 14.2 %all_to_all.26.amp_ref = bf16[128,4,128]{2,1,0:T(4,128)(2,1)S(1)} all-to-all(bf16[128,4,128]{2,1,0:T(4,128)(2,1)S(1)} %broadcast_in_dim.20), channel_id=1, replica_groups=mesh['row'=8,'col'=16] {'row','col'}, dimensions={0} | all-to-all | bytes 262144 | tf_op jit(solution)/shard_map/all_to_all | solution.py:25
  64.4 0.0 copy-start
  64.4 0.0 copy-start.1
  64.4 0.0 copy-start.2
  64.4 3.5 %shard_map.68 = bf16[128,4,128]{2,1,0:T(4,128)(2,1)S(1)} custom-call(bf16[128,4,128]{2,1,0:T(4,128)(2,1)S(1)} %all_to_all.26.amp_ref, bf16[1280,512]{1,0:T(8,128)(2,1)S(1)} %get-tuple-element.19.virt_ref, bf16[2560,128]{1,0:T(8,128)(2,1)S(1)} %shard_map.65.occ_ref, bf16[512,1280]{1,0:T(8,128)(2,1)S(1)} %shard_map.66.head_ref, ...), custom_call_target="tpu_custom_call" | custom-call | tf_op jit(solution)/shard_map/pallas_call | solution.py:245
  67.9 14.2 %all_to_all.27 = bf16[128,4,128]{2,1,0:T(4,128)(2,1)S(1)} all-to-all(bf16[128,4,128]{2,1,0:T(4,128)(2,1)S(1)} %shard_map.68), channel_id=1, replica_groups=mesh['row'=8,'col'=16] {'row','col'}, dimensions={0} | all-to-all | bytes 262144 | tf_op jit(solution)/shard_map/all_to_all | solution.py:273
  82.1 0.1 reduce_sum.22
  82.3 14.2 %all_to_all.28.blocks_ref = bf16[128,4,128]{2,1,0:T(4,128)(2,1)S(1)} all-to-all(bf16[128,4,128]{2,1,0:T(4,128)(2,1)S(1)} %broadcast_in_dim.21), channel_id=1, replica_groups=mesh['row'=8,'col'=16] {'row','col'}, dimensions={0} | all-to-all | bytes 262144 | tf_op jit(solution)/shard_map/all_to_all | solution.py:25
  96.4 0.0 copy-done
  96.4 0.0 copy-done.1
  96.4 0.0 copy-done.2
  96.4 0.9 shard_map.69
  (11 shorter events, 0.2 us)
Async XLA Ops:
  0.0 11.6 %collective-permute-start = (bf16[1,160,128]{2,1,0:T(8,128)(2,1)}, bf16[1,160,128]{2,1,0:T(8,128)(2,1)S(1)}, u32[]{:S(2)}, u32[]{:S(2)}) collective-permute-start(bf16[1,160,128]{2,1,0:T(8,128)(2,1)} %bitcast.12), channel_id=1, source_target_pairs={{0,8},{1,9},{2,10},{3,11},{4,12},{5,13},{6,14},{7,15},{8,0},{9,1},... | collective-permute-start | bytes 122888 | tf_op jit(solution)/shard_map/ppermute | solution.py:42
  6.5 20.5 %all-to-all-start = ((bf16[8,160,512]{2,1,0:T(8,128)(2,1)}), bf16[8,160,512]{2,1,0:T(8,128)(2,1)S(1)}, u32[]{:S(2)}, u32[]{:S(2)}) async-start(bf16[8,160,512]{2,1,0:T(8,128)(2,1)} %get-tuple-element.15), calls=%async_computation | async-start | bytes 2621440 | tf_op jit(solution)/shard_map/all_to_all | solution.py:58
  11.6 4.9 %collective-permute-start.1 = (bf16[2,160,128]{2,1,0:T(8,128)(2,1)S(1)}, bf16[2,160,128]{2,1,0:T(8,128)(2,1)S(1)}, u32[]{:S(2)}, u32[]{:S(2)}) collective-permute-start(bf16[2,160,128]{2,1,0:T(8,128)(2,1)S(1)} %pad_maximum_fusion.2), channel_id=1, source_target_pairs={{0,4},{1,5},{2,6},{3,7},{4,0},{5,1},{6,2},{7,3},{8,12},{9,13},{10,... | collective-permute-start | bytes 245768 | tf_op jit(solution)/shard_map/ppermute | solution.py:42
  16.5 4.5 %collective-permute-start.2 = (bf16[4,160,128]{2,1,0:T(8,128)(2,1)S(1)}, bf16[4,160,128]{2,1,0:T(8,128)(2,1)S(1)}, u32[]{:S(2)}, u32[]{:S(2)}) collective-permute-start(bf16[4,160,128]{2,1,0:T(8,128)(2,1)S(1)} %pad_maximum_fusion.1), channel_id=1, source_target_pairs={{0,2},{1,3},{2,0},{3,1},{4,6},{5,7},{6,4},{7,5},{8,10},{9,11},{10,... | collective-permute-start | bytes 491528 | tf_op jit(solution)/shard_map/ppermute | solution.py:42
  21.1 4.9 %collective-permute-start.3 = (bf16[8,160,128]{2,1,0:T(8,128)(2,1)S(1)}, bf16[8,160,128]{2,1,0:T(8,128)(2,1)S(1)}, u32[]{:S(2)}, u32[]{:S(2)}) collective-permute-start(bf16[8,160,128]{2,1,0:T(8,128)(2,1)S(1)} %pad_maximum_fusion), channel_id=1, source_target_pairs={{0,1},{1,0},{2,3},{3,2},{4,5},{5,4},{6,7},{7,6},{8,9},{9,8},{10,11... | collective-permute-start | bytes 983048 | tf_op jit(solution)/shard_map/ppermute | solution.py:42
  64.4 32.0 %copy-start = (f32[128,512]{1,0:T(8,128)S(1)}, f32[128,512]{1,0:T(8,128)}, u32[]{:S(2)}) copy-start(f32[128,512]{1,0:T(8,128)} %rhs_ref.3) | copy-start | bytes 786436
  64.4 32.0 %copy-start.1 = (f32[512]{0:T(512)S(1)}, f32[512]{0:T(512)}, u32[]{:S(2)}) copy-start(f32[512]{0:T(512)} %param.11) | copy-start | bytes 6148
  64.4 32.0 %copy-start.2 = (f32[128]{0:T(128)S(1)}, f32[128]{0:T(128)}, u32[]{:S(2)}) copy-start(f32[128]{0:T(128)} %param.10) | copy-start | bytes 1540
